TPU v7x, 32 devices: a whole 2x2x4 slice. The times are simulated.
32 devices in a mesh: term: 8 (over z, core), doc: 4 (over y, x).
Axes of the slice: x: 2, y: 2, z: 4, core: 2. Of those that a mesh axis runs over, the one named last changes fastest.
Arguments:
- tile_values: bfloat16 [384, 512, 128], P('term', 'doc'), may hold values from 0.001 to 1, as said below
- tile_rows: int32 [8, 192], P('term', 'doc'), may hold values from 0 to 15, as said below
- tile_cols: int32 [8, 192], P('term', 'doc'), may hold values from 0 to 15, as said below
- tile_count: int32 [8, 4], P('term', 'doc'), may hold values from 16 to 48, as said below
- start_block: bfloat16 [8192, 256], P('doc'), may hold values from -6 to 6
Outputs:
- row_scale: float32 [16384], P('term')
- col_scale: float32 [8192], P('doc')
- left_basis: bfloat16 [16384, 256], P('term')
- right_basis: bfloat16 [8192, 256], P('doc')
Inputs may be any that keep to these rules, and one draw needn't show every extreme that they name: `tile_values`: entries are positive. `tile_rows`: within one block pair the occupied (row, column) pairs are distinct, and every tile row and tile column of every block pair holds an occupied tile. `tile_cols`: paired with tile_rows slot by slot. `tile_count`: some block pair has all 48 slots occupied.
All inputs are finite; a program needn't handle non-finite values.
Results may differ from a plain program's by a relative error of at most 0.006.
The roundings to bfloat16 on the way count: a program that leaves them out, or rounds other values in their place, can miss the bound.
Values may be sent and summed in bfloat16 or wider, within the bound.
A program may use at most 64 MiB of HBM per device.

v0:
```python
import functools

import jax
import jax.numpy as jnp
from jax import lax
from jax.experimental import pallas as pl
from jax.experimental.pallas import tpu as pltpu
from jax.sharding import PartitionSpec as P

TILE = 128
PASSES = 2
RB = 16
CB = 16


PRECISE = lax.Precision.HIGHEST
MESH = pl.DeviceIdType.MESH
VMEM = pl.BlockSpec(memory_space=pltpu.VMEM)
SMEM = pl.BlockSpec(memory_space=pltpu.SMEM)


BLOCK = 64
GROUP = 8


def block_inverse(block, low, high):
    rows = lax.broadcasted_iota(jnp.int32, block.shape, 0)
    pivots = jnp.ones_like(block)
    for base in range(0, BLOCK, GROUP):
        factors = []
        for at in range(base, base + GROUP):
            column = jnp.broadcast_to(block[:, low + at : low + at + 1], block.shape)
            for past, factor in enumerate(factors):
                column = column - factor * column[base + past : base + past + 1, :]
            pivots = jnp.where(rows == at, column, pivots)
            ratio = column * (1.0 / column[at : at + 1, :])
            factors.append(jnp.where(rows > at, ratio, 0.0))
        for at, factor in enumerate(factors):
            block = block - factor * block[base + at : base + at + 1, :]
    lanes = lax.broadcasted_iota(jnp.int32, block.shape, 1)
    inside = (lanes >= high) & (lanes < high + BLOCK)
    return jnp.where(inside, block * lax.rsqrt(pivots), 0.0)


def inverse_kernel(gram_ref, o_ref, work):
    width = gram_ref.shape[0]
    work[:, :width] = gram_ref[...]
    rows = lax.broadcasted_iota(jnp.int32, (width, width), 0)
    lanes = lax.broadcasted_iota(jnp.int32, (width, width), 1)
    work[:, width:] = jnp.where(rows == lanes, 1.0, 0.0)
    for index in range(width // BLOCK):
        start = index * BLOCK
        near = start // TILE * TILE
        low = start - near
        high = TILE - BLOCK - low
        block = work[start : start + BLOCK, near : near + TILE]
        rows = lax.broadcasted_iota(jnp.int32, block.shape, 0)
        lanes = lax.broadcasted_iota(jnp.int32, block.shape, 1)
        inside = (lanes >= low) & (lanes < low + BLOCK)
        block = jnp.where(inside, block, jnp.where(lanes - high == rows, 1.0, 0.0))
        inverse = block_inverse(block, low, high)
        panel = work[start : start + BLOCK, :]
        solved = jnp.dot(
            inverse,
            jnp.concatenate([panel, panel], axis=0),
            precision=PRECISE,
            preferred_element_type=jnp.float32,
        )
        o_ref[start : start + BLOCK, :] = solved[:, width:]
        if start + BLOCK < width:
            update = lax.dot_general(
                solved[:, :width],
                solved,
                (((0,), (0,)), ((), ())),
                precision=PRECISE,
                preferred_element_type=jnp.float32,
            )
            work[start + BLOCK :, :] = work[start + BLOCK :, :] - update[start + BLOCK :, :]


def factor_inverse(gram):
    width = gram.shape[0]
    return pl.pallas_call(
        inverse_kernel,
        out_shape=jax.ShapeDtypeStruct(gram.shape, gram.dtype),
        in_specs=[VMEM],
        out_specs=VMEM,
        scratch_shapes=[pltpu.VMEM((width, 2 * width), jnp.float32)],
        compiler_params=pltpu.CompilerParams(vmem_limit_bytes=16 << 20),
        name="inverse",
    )(gram).T


def params(identifier):
    return pltpu.CompilerParams(
        collective_id=identifier, has_side_effects=True, vmem_limit_bytes=32 << 20
    )


def greet(axes):
    barrier = pltpu.get_barrier_semaphore()
    total = 0
    for axis in axes:
        n = lax.axis_size(axis)
        me = lax.axis_index(axis)
        for step in range(1, n):
            pl.semaphore_signal(
                barrier, inc=1, device_id={axis: lax.rem(me + step, n)}, device_id_type=MESH
            )
        total += n - 1
    pl.semaphore_wait(barrier, total)


def remote(source, target, send_sem, recv_sem, axis, peer):
    return pltpu.make_async_remote_copy(
        src_ref=source,
        dst_ref=target,
        send_sem=send_sem,
        recv_sem=recv_sem,
        device_id={axis: peer},
        device_id_type=MESH,
    )


def all_sum_kernel(axis, x_ref, o_ref, held, send_sem, recv_sem):
    n = lax.axis_size(axis)
    me = lax.axis_index(axis)
    greet((axis,))
    copies = []
    for step in range(1, n):
        copy = remote(
            x_ref, held.at[step], send_sem.at[step], recv_sem.at[step], axis, lax.rem(me + step, n)
        )
        copy.start()
        copies.append(copy)
    held[0] = x_ref[...]
    for copy in copies:
        copy.wait()
    total = held[me]
    for source in range(1, n):
        total = total + held[lax.rem(me - source + n, n)]
    o_ref[...] = total


def all_sum(x, axis, identifier):
    n = lax.axis_size(axis)
    return pl.pallas_call(
        functools.partial(all_sum_kernel, axis),
        out_shape=jax.ShapeDtypeStruct(x.shape, x.dtype),
        in_specs=[VMEM],
        out_specs=VMEM,
        scratch_shapes=[
            pltpu.VMEM((n,) + x.shape, x.dtype),
            pltpu.SemaphoreType.DMA((n,)),
            pltpu.SemaphoreType.DMA((n,)),
        ],
        compiler_params=params(identifier),
        name="all_sum",
    )(x)


def scatter_sum_kernel(axis, x_ref, o_ref, held, send_sem, recv_sem):
    n = lax.axis_size(axis)
    me = lax.axis_index(axis)
    greet((axis,))
    copies = []
    for step in range(1, n):
        peer = lax.rem(me + step, n)
        copy = remote(
            x_ref.at[peer], held.at[step], send_sem.at[step], recv_sem.at[step], axis, peer
        )
        copy.start()
        copies.append(copy)
    o_ref[...] = x_ref[me]
    for step, copy in enumerate(copies):
        copy.wait()
        o_ref[...] += held[step + 1]


def scatter_sum(x, axis, identifier):
    n = lax.axis_size(axis)
    return pl.pallas_call(
        functools.partial(scatter_sum_kernel, axis),
        out_shape=jax.ShapeDtypeStruct(x.shape[1:], x.dtype),
        in_specs=[VMEM],
        out_specs=VMEM,
        scratch_shapes=[
            pltpu.VMEM(x.shape, x.dtype),
            pltpu.SemaphoreType.DMA((n,)),
            pltpu.SemaphoreType.DMA((n,)),
        ],
        compiler_params=params(identifier),
        name="scatter_sum",
    )(x)


def gather_kernel(axis, x_ref, o_ref, send_sem, recv_sem):
    n = lax.axis_size(axis)
    me = lax.axis_index(axis)
    greet((axis,))
    copies = []
    for step in range(1, n):
        copy = remote(
            x_ref, o_ref.at[me], send_sem.at[step], recv_sem.at[step], axis, lax.rem(me + step, n)
        )
        copy.start()
        copies.append(copy)
    o_ref[me] = x_ref[...]
    for copy in copies:
        copy.wait()


def gather(x, axis, identifier):
    n = lax.axis_size(axis)
    return pl.pallas_call(
        functools.partial(gather_kernel, axis),
        out_shape=jax.ShapeDtypeStruct((n,) + x.shape, x.dtype),
        in_specs=[VMEM],
        out_specs=VMEM,
        scratch_shapes=[
            pltpu.SemaphoreType.DMA((n,)),
            pltpu.SemaphoreType.DMA((n,)),
        ],
        compiler_params=params(identifier),
        name="gather",
    )(x)


def gram_sum_kernel(x_ref, o_ref, first, second, part, done, *sems):
    n, m = lax.axis_size("term"), lax.axis_size("doc")
    me, my = lax.axis_index("term"), lax.axis_index("doc")
    send_a, recv_a, send_b, recv_b, send_c, recv_c = sems
    greet(("term", "doc"))
    copies = []
    for step in range(1, n):
        peer = lax.rem(me + step, n)
        copy = remote(x_ref.at[peer], first.at[step], send_a.at[step], recv_a.at[step], "term", peer)
        copy.start()
        copies.append(copy)
    part[...] = x_ref[me]
    for step, copy in enumerate(copies):
        copy.wait()
        part[...] += first[step + 1]
    copies = []
    for step in range(1, m):
        copy = remote(
            part, second.at[step], send_b.at[step], recv_b.at[step], "doc", lax.rem(my + step, m)
        )
        copy.start()
        copies.append(copy)
    second[0] = part[...]
    for copy in copies:
        copy.wait()
    total = second[my]
    for source in range(1, m):
        total = total + second[lax.rem(my - source + m, m)]
    done[...] = total
    copies = []
    for step in range(1, n):
        copy = remote(
            done, o_ref.at[me], send_c.at[step], recv_c.at[step], "term", lax.rem(me + step, n)
        )
        copy.start()
        copies.append(copy)
    o_ref[me] = done[...]
    for copy in copies:
        copy.wait()


def gram_sum(x, identifier):
    n, m = lax.axis_size("term"), lax.axis_size("doc")
    share = x.shape[1:]
    return pl.pallas_call(
        gram_sum_kernel,
        out_shape=jax.ShapeDtypeStruct(x.shape, x.dtype),
        in_specs=[VMEM],
        out_specs=VMEM,
        scratch_shapes=[
            pltpu.VMEM((n,) + share, x.dtype),
            pltpu.VMEM((m,) + share, x.dtype),
            pltpu.VMEM(share, x.dtype),
            pltpu.VMEM(share, x.dtype),
        ]
        + [pltpu.SemaphoreType.DMA((size,)) for size in (n, n, m, m, n, n)],
        compiler_params=params(identifier),
        name="gram_sum",
    )(x)


def dense_kernel(rows_ref, cols_ref, count_ref, tiles_ref, o_ref, t_ref):
    def clear(index, carry):
        at = pl.multiple_of(index * 32, 32)
        o_ref[pl.ds(at, 32), :] = jnp.zeros((32, o_ref.shape[1]), o_ref.dtype)
        t_ref[pl.ds(at, 32), :] = jnp.zeros((32, t_ref.shape[1]), t_ref.dtype)
        return carry

    lax.fori_loop(0, o_ref.shape[0] // 32, clear, 0)

    def place(slot, carry):
        row = pl.multiple_of(rows_ref[0, slot] * TILE, TILE)
        col = pl.multiple_of(cols_ref[0, slot] * TILE, TILE)
        tile = tiles_ref[slot]
        o_ref[pl.ds(row, TILE), pl.ds(col, TILE)] = tile
        t_ref[pl.ds(col, TILE), pl.ds(row, TILE)] = tile.T
        return carry

    lax.fori_loop(0, count_ref[0, 0], place, 0)


def dense_matrix(tile_values, tile_rows, tile_cols, tile_count):
    return pl.pallas_call(
        dense_kernel,
        out_shape=[
            jax.ShapeDtypeStruct((RB * TILE, CB * TILE), tile_values.dtype),
            jax.ShapeDtypeStruct((CB * TILE, RB * TILE), tile_values.dtype),
        ],
        in_specs=[SMEM, SMEM, SMEM, VMEM],
        out_specs=[VMEM, VMEM],
        compiler_params=pltpu.CompilerParams(vmem_limit_bytes=32 << 20),
        name="dense",
    )(tile_rows, tile_cols, tile_count, tile_values)


def row_sums(matrix, scale):
    return jnp.sum(matrix.astype(jnp.float32) * scale[None, :], axis=1)


def col_sums(matrix, scale):
    return jnp.sum(matrix.astype(jnp.float32) * scale[:, None], axis=0)


def vector_sum(x, axis, identifier):
    return all_sum(x.reshape(-1, TILE), axis, identifier).reshape(-1)


def total_gram(block, extra, scale, identifier):
    n = lax.axis_size("term")
    width = block.shape[1]
    gram = jnp.dot(block.T, block, precision=PRECISE) / scale
    rows = [gram]
    if extra is not None:
        rows += [extra[None, :], jnp.zeros((8 * n - 1, width), jnp.float32)]
    stacked = jnp.concatenate(rows, axis=0) if extra is not None else gram
    summed = gram_sum(stacked.reshape(n, -1, width), identifier).reshape(stacked.shape)
    return summed[:width], (summed[width] if extra is not None else None)


def per_device(tile_values, tile_rows, tile_cols, tile_count, start_block):
    terms_total = RB * TILE * lax.axis_size("term")
    docs_total = CB * TILE * lax.axis_size("doc")
    width = start_block.shape[1]
    matrix, turned = dense_matrix(tile_values, tile_rows, tile_cols, tile_count)

    mean_part = jnp.sum(start_block.astype(jnp.float32), axis=0)
    col_flat = jnp.ones((CB * TILE,), jnp.float32)
    for sweep_index in range(PASSES):
        row_part = row_sums(matrix, col_flat)
        if sweep_index == 0:
            pad = jnp.zeros((8 * TILE - width % (8 * TILE),), jnp.float32)
            joined = vector_sum(jnp.concatenate([row_part, mean_part, pad]), "doc", 0)
            row_total = joined[: RB * TILE]
            start_mean = joined[RB * TILE : RB * TILE + width]
        else:
            row_total = vector_sum(row_part, "doc", 1 + 2 * sweep_index)
        row_flat = 1.0 / row_total
        col_part = col_sums(matrix, row_flat)
        col_flat = 1.0 / vector_sum(col_part, "term", 2 + 2 * sweep_index)
    scaled_start = (col_flat[:, None] * start_block.astype(jnp.float32)).astype(jnp.bfloat16)
    left_part = jnp.dot(matrix, scaled_start, preferred_element_type=jnp.float32)
    doc_size = lax.axis_size("doc")
    left_share = RB * TILE // doc_size
    left_offset = lax.axis_index("doc") * left_share
    weight_sum = vector_sum(row_sums(matrix, col_flat), "doc", 16)
    left_raw = scatter_sum(left_part.reshape(doc_size, left_share, width), "doc", 17)
    row_rows = lax.dynamic_slice_in_dim(row_flat, left_offset, left_share)
    row_weight = row_rows * lax.dynamic_slice_in_dim(weight_sum, left_offset, left_share)
    left_block = (
        row_rows[:, None] * left_raw - row_weight[:, None] * start_mean[None, :] / docs_total
    )
    weighted = jnp.sum(row_weight[:, None] * left_block, axis=0)
    left_gram, weighted = total_gram(left_block, weighted, terms_total, 18)
    left_inverse = factor_inverse(left_gram)
    share_float = jnp.dot(left_block, left_inverse, precision=PRECISE)
    lean = jnp.dot(weighted, left_inverse, precision=PRECISE)
    left_basis = gather(share_float.astype(jnp.bfloat16), "doc", 19).reshape(RB * TILE, width)
    scaled_left = (row_flat[:, None] * left_basis.astype(jnp.float32)).astype(jnp.bfloat16)
    right_part = jnp.dot(turned, scaled_left, preferred_element_type=jnp.float32)
    term_size = lax.axis_size("term")
    right_share = CB * TILE // term_size
    right_offset = lax.axis_index("term") * right_share
    right_raw = scatter_sum(right_part.reshape(term_size, right_share, width), "term", 20)
    col_rows = lax.dynamic_slice_in_dim(col_flat, right_offset, right_share)
    right_block = col_rows[:, None] * right_raw - lean[None, :] / docs_total
    right_gram, _ = total_gram(right_block, None, docs_total, 21)
    right_inverse = factor_inverse(right_gram)
    right_piece = jnp.dot(right_block, right_inverse, precision=PRECISE).astype(jnp.bfloat16)
    right_basis = gather(right_piece, "term", 22).reshape(CB * TILE, width)
    return (row_flat, col_flat, left_basis, right_basis)


def solution(mesh):
    placed = (
        P("term", "doc", None),
        P("term", "doc"),
        P("term", "doc"),
        P("term", "doc"),
        P("doc", None),
    )
    return jax.shard_map(
        per_device,
        mesh=mesh,
        in_specs=placed,
        out_specs=(P("term"), P("doc"), P("term", None), P("doc", None)),
        check_vma=False,
    )
```

profile of v0, /device:TPU:9, one launch (start us, length us, event | category | flops | bytes accessed | tf_op | source)
XLA Modules:
  0.0 240.8 jit_solution(11788919499367976559)
XLA Ops:
  1.3 1.5 convert_reduce_fusion.1
  2.9 1.4 copy-done.2
  5.6 3.2 %dense.1 = (bf16[2048,2048]{1,0:T(8,128)(2,1)S(1)}, bf16[2048,2048]{1,0:T(8,128)(2,1)S(1)}) custom-call(s32[1,48]{1,0:T(1,128)S(1)} %copy-done.3, s32[1,48]{1,0:T(1,128)S(1)} %copy-done.4, s32[1,1]{1,0:T(1,128)S(6)} %copy.11.count_ref, bf16[48,128,128]{2,1,0:T(8,128)(2,1)S(1)} %copy-done.2), custom_call_target="tpu_custom_call" | custom-call | tf_op jit(solution)/shard_map/dense/pallas_call | solution.py:311
  8.9 3.2 %copy-done.5 = bf16[2048,2048]{1,0:T(8,128)(2,1)} copy-done((bf16[2048,2048]{1,0:T(8,128)(2,1)}, bf16[2048,2048]{1,0:T(8,128)(2,1)S(1)}, u32[]{:S(2)}) %copy-start.5) | copy-done | bytes 8388632
  13.3 4.3 %all_sum.5 = f32[24,128]{1,0:T(8,128)S(1)} custom-call(f32[24,128]{1,0:T(8,128)S(1)} %maximum_bitcast_fusion.x_ref), custom_call_target="tpu_custom_call" | custom-call | tf_op jit(solution)/shard_map/all_sum/pallas_call | solution.py:147
  17.6 1.7 fusion
  19.3 8.0 %all_sum.6 = f32[16,128]{1,0:T(8,128)S(1)} custom-call(f32[16,128]{1,0:T(8,128)S(1)} %bitcast.51), custom_call_target="tpu_custom_call" | custom-call | tf_op jit(solution)/shard_map/all_sum/pallas_call | solution.py:147
  27.3 1.7 fusion.1
  29.0 3.5 %all_sum.7 = f32[16,128]{1,0:T(8,128)S(1)} custom-call(f32[16,128]{1,0:T(8,128)S(1)} %bitcast.52), custom_call_target="tpu_custom_call" | custom-call | tf_op jit(solution)/shard_map/all_sum/pallas_call | solution.py:147
  32.7 5.2 %fusion.2 = f32[2048]{0:T(1024)S(1)} fusion(bf16[2048,2048]{1,0:T(8,128)(2,1)} %copy-done, f32[2048]{0:T(1024)S(1)} %get-tuple-element.16), kind=kLoop, calls=%fused_computation.7 | loop fusion | flops 12580864 | bytes 8404992 | tf_op jit(solution)/shard_map/reduce_sum | solution.py:329
  37.9 7.2 %all_sum.8 = f32[16,128]{1,0:T(8,128)S(1)} custom-call(f32[16,128]{1,0:T(8,128)S(1)} %bitcast.53), custom_call_target="tpu_custom_call" | custom-call | tf_op jit(solution)/shard_map/all_sum/pallas_call | solution.py:147
  45.2 1.7 fusion.3
  46.9 2.6 %fusion.5 = f32[2048,256]{1,0:T(8,128)S(1)} fusion(bf16[2048,2048]{1,0:T(8,128)(2,1)S(1)} %copy-done.1, bf16[2048,256]{1,0:T(8,128)(2,1)S(1)} %copy-done.6, f32[2048]{0:T(1024)S(1)} %divide_bitcast_fusion), kind=kOutput, calls=%fused_computation.17 | convolution fusion | flops 2149056512 | bytes 11542528 | tf_op jit(solution)/shard_map/dot_general | solution.py:369
  49.5 25.2 %scatter_sum.2 = f32[512,256]{1,0:T(8,128)S(1)} custom-call(f32[4,512,256]{2,1,0:T(8,128)S(1)} %bitcast.44), custom_call_target="tpu_custom_call" | custom-call | tf_op jit(solution)/shard_map/scatter_sum/pallas_call | solution.py:182
  74.7 3.5 %all_sum.9 = f32[16,128]{1,0:T(8,128)S(1)} custom-call(f32[16,128]{1,0:T(8,128)S(1)} %bitcast.50), custom_call_target="tpu_custom_call" | custom-call | tf_op jit(solution)/shard_map/all_sum/pallas_call | solution.py:147
  78.6 1.5 convolution_multiply_fusion.1
  80.2 24.2 %gram_sum.2 = f32[8,40,256]{2,1,0:T(8,128)S(1)} custom-call(f32[8,40,256]{2,1,0:T(8,128)S(1)} %bitcast.45), custom_call_target="tpu_custom_call" | custom-call | tf_op jit(solution)/shard_map/gram_sum/pallas_call | solution.py:273
  104.4 9.4 %inverse.2 = f32[256,256]{1,0:T(8,128)S(1)} custom-call(f32[256,256]{1,0:T(8,128)S(1)} %slice.18.gram_ref), custom_call_target="tpu_custom_call" | custom-call | tf_op jit(solution)/shard_map/inverse/pallas_call | solution.py:83
  114.7 14.2 %gather.2 = bf16[4,512,256]{2,1,0:T(8,128)(2,1)S(1)} custom-call(bf16[512,256]{1,0:T(8,128)(2,1)S(1)} %convolution_convert_fusion.x_ref), custom_call_target="tpu_custom_call" | custom-call | tf_op jit(solution)/shard_map/gather/pallas_call | solution.py:215
  129.3 2.5 %fusion.26.x_ref = f32[8,256,256]{2,1,0:T(8,128)S(1)} fusion(bf16[8,256,2048]{2,1,0:T(8,128)(2,1)S(1)} %bitcast.57, bf16[2048,256,1]{1,0,2:T(8,128)(2,1)S(1)} %bitcast.58), kind=kOutput, calls=%fused_computation.50 | convolution fusion | flops 2147483648 | bytes 11534336 | tf_op jit(solution)/shard_map/dot_general | solution.py:387
  131.8 50.4 %scatter_sum.3 = f32[256,256]{1,0:T(8,128)S(1)} custom-call(f32[8,256,256]{2,1,0:T(8,128)S(1)} %fusion.26.x_ref), custom_call_target="tpu_custom_call" | custom-call | tf_op jit(solution)/shard_map/scatter_sum/pallas_call | solution.py:182
  183.2 19.6 %gram_sum.3 = f32[8,32,256]{2,1,0:T(8,128)S(1)} custom-call(f32[8,32,256]{2,1,0:T(8,128)S(1)} %bitcast.49), custom_call_target="tpu_custom_call" | custom-call | tf_op jit(solution)/shard_map/gram_sum/pallas_call | solution.py:273
  202.8 9.4 %inverse.3 = f32[256,256]{1,0:T(8,128)S(1)} custom-call(f32[256,256]{1,0:T(8,128)S(1)} %bitcast.48), custom_call_target="tpu_custom_call" | custom-call | tf_op jit(solution)/shard_map/inverse/pallas_call | solution.py:83
  212.6 26.3 %gather.3 = bf16[8,256,256]{2,1,0:T(8,128)(2,1)S(1)} custom-call(bf16[256,256]{1,0:T(8,128)(2,1)S(1)} %convolution_convert_fusion.1.x_ref), custom_call_target="tpu_custom_call" | custom-call | tf_op jit(solution)/shard_map/gather/pallas_call | solution.py:215
  (45 shorter events, 7.7 us)
Async XLA Ops:
  2.9 1.4 copy-start.2
  4.3 0.7 copy-start.3
  4.9 0.7 copy-start.4
  8.9 3.2 %copy-start.5 = (bf16[2048,2048]{1,0:T(8,128)(2,1)}, bf16[2048,2048]{1,0:T(8,128)(2,1)S(1)}, u32[]{:S(2)}) copy-start(bf16[2048,2048]{1,0:T(8,128)(2,1)S(1)} %get-tuple-element.7) | copy-start | bytes 25165828
  12.1 15.2 %copy-start = (bf16[2048,2048]{1,0:T(8,128)(2,1)}, bf16[2048,2048]{1,0:T(8,128)(2,1)S(1)}, u32[]{:S(2)}) copy-start(bf16[2048,2048]{1,0:T(8,128)(2,1)S(1)} %get-tuple-element.6) | copy-start | bytes 25165828
  32.6 45.7 %copy-start.7 = (f32[2048]{0:T(1024)}, f32[2048]{0:T(1024)S(1)}, u32[]{:S(2)}) copy-start(f32[2048]{0:T(1024)S(1)} %get-tuple-element.16) | copy-start | bytes 24580
  32.6 12.5 %copy-start.1 = (bf16[2048,2048]{1,0:T(8,128)(2,1)S(1)}, bf16[2048,2048]{1,0:T(8,128)(2,1)}, u32[]{:S(2)}) copy-start(bf16[2048,2048]{1,0:T(8,128)(2,1)} %copy-done) | copy-start | bytes 25165828
  32.6 14.2 %copy-start.6 = (bf16[2048,256]{1,0:T(8,128)(2,1)S(1)}, bf16[2048,256]{1,0:T(8,128)(2,1)}, u32[]{:S(2)}) copy-start(bf16[2048,256]{1,0:T(8,128)(2,1)} %param.9) | copy-start | bytes 3145732
  45.1 4.4 %copy-start.8 = (f32[2048]{0:T(1024)}, f32[2048]{0:T(1024)S(1)}, u32[]{:S(2)}) copy-start(f32[2048]{0:T(1024)S(1)} %divide_bitcast_fusion) | copy-start | bytes 24580
  45.1 84.2 %slice-start = ((s8[8388608]{0:T(1024)(128)(4,1)}), s8[4194304]{0:T(1024)(128)(4,1)S(1)}, s32[]{:S(2)}) async-start(s8[8388608]{0:T(1024)(128)(4,1)} %bitcast.55), calls=%async_computation | async-start | bytes 8388608
  46.9 82.4 %slice-start.1 = ((s8[8388608]{0:T(1024)(128)(4,1)}), s8[4194304]{0:T(1024)(128)(4,1)S(1)}, s32[]{:S(2)}) async-start(s8[8388608]{0:T(1024)(128)(4,1)} %bitcast.55), calls=%async_computation.1 | async-start | bytes 8388608
where the time goes:
time: 241 us
  Pallas kernels  208 us (86%)
  other arithmetic  13.8 us (6%)
  matrix products  8.81 us (4%)
  local copies, waits for them, and re-layouts  8.1 us (3%)
    pallas_call x2, Pallas kernels, scatter_sum(): pl.pallas_call(functools.partial(scatter_sum_kernel, axis), out_shape=jax...  75.7 us
    pallas_call x2, Pallas kernels, gram_sum(): pl.pallas_call(gram_sum_kernel, out_shape=jax.ShapeDtypeStruct(x.shape, x...  43.8 us
    pallas_call x2, Pallas kernels, gather(): pl.pallas_call(functools.partial(gather_kernel, axis), out_shape=jax.Shap...  40.5 us
    pallas_call x5, Pallas kernels, all_sum(): pl.pallas_call(functools.partial(all_sum_kernel, axis), out_shape=jax.Sha...  26.5 us
    pallas_call x2, Pallas kernels, factor_inverse(): pl.pallas_call(inverse_kernel, out_shape=jax.ShapeDtypeStruct(gram.shape,...  18.7 us
    unnamed x24, local copies, waits for them, and re-layouts  7.91 us
    reduce_sum x2, other arithmetic, col_sums(): return jnp.sum(matrix.astype(jnp.float32) * scale[:, None], axis=0)  6.92 us

commit v1 on v0

--- a/solution.py
+++ b/solution.py
@@ -226,21 +226,130 @@
     )(x)
 
 
-def gram_sum_kernel(x_ref, o_ref, first, second, part, done, *sems):
-    n, m = lax.axis_size("term"), lax.axis_size("doc")
-    me, my = lax.axis_index("term"), lax.axis_index("doc")
-    send_a, recv_a, send_b, recv_b, send_c, recv_c = sems
-    greet(("term", "doc"))
-    copies = []
-    for step in range(1, n):
-        peer = lax.rem(me + step, n)
-        copy = remote(x_ref.at[peer], first.at[step], send_a.at[step], recv_a.at[step], "term", peer)
-        copy.start()
-        copies.append(copy)
-    part[...] = x_ref[me]
-    for step, copy in enumerate(copies):
+def paired():
+    n, me = lax.axis_size("term"), lax.axis_index("term")
+    return n // 2, me // 2, lax.rem(me, 2)
+
+
+def greet_paired(with_doc):
+    nz, z, c = paired()
+    barrier = pltpu.get_barrier_semaphore()
+    targets = [("term", 2 * z + 1 - c)]
+    targets += [("term", 2 * lax.rem(z + step, nz) + c) for step in range(1, nz)]
+    if with_doc:
+        m, my = lax.axis_size("doc"), lax.axis_index("doc")
+        targets += [("doc", lax.rem(my + step, m)) for step in range(1, m)]
+    for axis, peer in targets:
+        pl.semaphore_signal(barrier, inc=1, device_id={axis: peer}, device_id_type=MESH)
+    pl.semaphore_wait(barrier, len(targets))
+
+
+def scatter_paired(x_ref, near, mid, far, total_ref, near_send, near_recv, far_send, far_recv):
+    nz, z, c = paired()
+    order = list(range(1, nz)) + [0]
+    near_copies = {}
+    for step in order:
+        near_copies[step] = remote(
+            x_ref.at[lax.rem(z + step, nz), 1 - c],
+            near.at[step],
+            near_send.at[step],
+            near_recv.at[step],
+            "term",
+            2 * z + 1 - c,
+        )
+        near_copies[step].start()
+    far_copies = []
+    for step in range(1, nz):
+        near_copies[step].wait()
+        there = lax.rem(z + step, nz)
+        mid[step] = x_ref[there, c] + near[step]
+        copy = remote(
+            mid.at[step], far.at[step], far_send.at[step], far_recv.at[step], "term", 2 * there + c
+        )
+        copy.start()
+        far_copies.append(copy)
+    near_copies[0].wait()
+    total_ref[...] = x_ref[z, c] + near[0]
+    for step, copy in enumerate(far_copies):
         copy.wait()
-        part[...] += first[step + 1]
+        total_ref[...] += far[step + 1]
+
+
+def gather_paired(x_ref, o_ref, near_send, near_recv, far_send, far_recv):
+    nz, z, c = paired()
+    sibling = 2 * z + 1 - c
+    far_copies = []
+    for step in range(1, nz):
+        copy = remote(
+            x_ref,
+            o_ref.at[z, c],
+            far_send.at[step],
+            far_recv.at[step],
+            "term",
+            2 * lax.rem(z + step, nz) + c,
+        )
+        copy.start()
+        far_copies.append(copy)
+    copy = remote(x_ref, o_ref.at[z, c], near_send.at[0], near_recv.at[0], "term", sibling)
+    copy.start()
+    near_copies = [copy]
+    o_ref[z, c] = x_ref[...]
+    for step in range(1, nz):
+        far_copies[step - 1].wait()
+        here = o_ref.at[lax.rem(z - step + nz, nz), c]
+        copy = remote(here, here, near_send.at[step], near_recv.at[step], "term", sibling)
+        copy.start()
+        near_copies.append(copy)
+    for copy in near_copies:
+        copy.wait()
+
+
+def semaphores(*sizes):
+    return [pltpu.SemaphoreType.DMA((size,)) for size in sizes]
+
+
+def scatter_term_kernel(x_ref, o_ref, near, mid, far, *sems):
+    greet_paired(False)
+    scatter_paired(x_ref, near, mid, far, o_ref, *sems)
+
+
+def scatter_term(x, identifier):
+    nz = x.shape[0]
+    share = x.shape[2:]
+    return pl.pallas_call(
+        scatter_term_kernel,
+        out_shape=jax.ShapeDtypeStruct(share, x.dtype),
+        in_specs=[VMEM],
+        out_specs=VMEM,
+        scratch_shapes=[pltpu.VMEM((nz,) + share, x.dtype)] * 3 + semaphores(nz, nz, nz, nz),
+        compiler_params=params(identifier),
+        name="scatter_term",
+    )(x)
+
+
+def gather_term_kernel(x_ref, o_ref, *sems):
+    greet_paired(False)
+    gather_paired(x_ref, o_ref, *sems)
+
+
+def gather_term(x, identifier):
+    nz = lax.axis_size("term") // 2
+    return pl.pallas_call(
+        gather_term_kernel,
+        out_shape=jax.ShapeDtypeStruct((nz, 2) + x.shape, x.dtype),
+        in_specs=[VMEM],
+        out_specs=VMEM,
+        scratch_shapes=semaphores(nz, nz, nz, nz),
+        compiler_params=params(identifier),
+        name="gather_term",
+    )(x)
+
+
+def gram_sum_kernel(x_ref, o_ref, near, mid, far, second, part, done, *sems):
+    m, my = lax.axis_size("doc"), lax.axis_index("doc")
+    send_b, recv_b = sems[4:6]
+    greet_paired(True)
+    scatter_paired(x_ref, near, mid, far, part, *sems[:4])
     copies = []
     for step in range(1, m):
         copy = remote(
@@ -255,33 +364,24 @@
     for source in range(1, m):
         total = total + second[lax.rem(my - source + m, m)]
     done[...] = total
-    copies = []
-    for step in range(1, n):
-        copy = remote(
-            done, o_ref.at[me], send_c.at[step], recv_c.at[step], "term", lax.rem(me + step, n)
-        )
-        copy.start()
-        copies.append(copy)
-    o_ref[me] = done[...]
-    for copy in copies:
-        copy.wait()
+    gather_paired(done, o_ref, *sems[6:])
 
 
 def gram_sum(x, identifier):
-    n, m = lax.axis_size("term"), lax.axis_size("doc")
-    share = x.shape[1:]
+    nz, m = x.shape[0], lax.axis_size("doc")
+    share = x.shape[2:]
     return pl.pallas_call(
         gram_sum_kernel,
         out_shape=jax.ShapeDtypeStruct(x.shape, x.dtype),
         in_specs=[VMEM],
         out_specs=VMEM,
-        scratch_shapes=[
-            pltpu.VMEM((n,) + share, x.dtype),
+        scratch_shapes=[pltpu.VMEM((nz,) + share, x.dtype)] * 3
+        + [
             pltpu.VMEM((m,) + share, x.dtype),
             pltpu.VMEM(share, x.dtype),
             pltpu.VMEM(share, x.dtype),
         ]
-        + [pltpu.SemaphoreType.DMA((size,)) for size in (n, n, m, m, n, n)],
+        + semaphores(nz, nz, nz, nz, m, m, nz, nz, nz, nz),
         compiler_params=params(identifier),
         name="gram_sum",
     )(x)
@@ -341,7 +441,7 @@
     if extra is not None:
         rows += [extra[None, :], jnp.zeros((8 * n - 1, width), jnp.float32)]
     stacked = jnp.concatenate(rows, axis=0) if extra is not None else gram
-    summed = gram_sum(stacked.reshape(n, -1, width), identifier).reshape(stacked.shape)
+    summed = gram_sum(stacked.reshape(n // 2, 2, -1, width), identifier).reshape(stacked.shape)
     return summed[:width], (summed[width] if extra is not None else None)
 
 
@@ -388,13 +488,13 @@
     term_size = lax.axis_size("term")
     right_share = CB * TILE // term_size
     right_offset = lax.axis_index("term") * right_share
-    right_raw = scatter_sum(right_part.reshape(term_size, right_share, width), "term", 20)
+    right_raw = scatter_term(right_part.reshape(term_size // 2, 2, right_share, width), 20)
     col_rows = lax.dynamic_slice_in_dim(col_flat, right_offset, right_share)
     right_block = col_rows[:, None] * right_raw - lean[None, :] / docs_total
     right_gram, _ = total_gram(right_block, None, docs_total, 21)
     right_inverse = factor_inverse(right_gram)
     right_piece = jnp.dot(right_block, right_inverse, precision=PRECISE).astype(jnp.bfloat16)
-    right_basis = gather(right_piece, "term", 22).reshape(CB * TILE, width)
+    right_basis = gather_term(right_piece, 22).reshape(CB * TILE, width)
     return (row_flat, col_flat, left_basis, right_basis)
 
 

time: 241 us -> 204 us (0.85)
  Pallas kernels: 208 us -> 172 us
    pallas_call x2 -> x1, Pallas kernels: 75.7 us -> 26.2 us  [scatter_sum(): pl.pallas_call(functools.partial(scatter_sum_kernel, axis), out_shape=jax...]
    pallas_call x0 -> x2, Pallas kernels: none -> 44.4 us  [the longest x1 28.4 us: scatter_term(): pl.pallas_call(scatter_term_kernel, out_shape=jax.ShapeDtypeStruct(share,...]
    pallas_call x2 -> x1, Pallas kernels: 40.5 us -> 13.8 us  [gather(): pl.pallas_call(functools.partial(gather_kernel, axis), out_shape=jax.Shap...]
    pallas_call x2, Pallas kernels: 43.8 us -> 38.4 us  [gram_sum(): pl.pallas_call(gram_sum_kernel, out_shape=jax.ShapeDtypeStruct(x.shape, x...]
where the time goes in v1:
time: 204 us; the launch traced here: 205 us
  Pallas kernels  172 us (84%)
  other arithmetic  13.8 us (7%)
  matrix products  8.81 us (4%)
  local copies, waits for them, and re-layouts  8.1 us (4%)
    pallas_call x2, Pallas kernels, gram_sum(): pl.pallas_call(gram_sum_kernel, out_shape=jax.ShapeDtypeStruct(x.shape, x...  38.4 us
    pallas_call x1, Pallas kernels, scatter_term(): pl.pallas_call(scatter_term_kernel, out_shape=jax.ShapeDtypeStruct(share,...  28.4 us
    pallas_call x5, Pallas kernels, all_sum(): pl.pallas_call(functools.partial(all_sum_kernel, axis), out_shape=jax.Sha...  26.9 us
    pallas_call x1, Pallas kernels, scatter_sum(): pl.pallas_call(functools.partial(scatter_sum_kernel, axis), out_shape=jax...  26.2 us
    pallas_call x2, Pallas kernels, factor_inverse(): pl.pallas_call(inverse_kernel, out_shape=jax.ShapeDtypeStruct(gram.shape,...  18.7 us
    pallas_call x1, Pallas kernels, gather_term(): pl.pallas_call(gather_term_kernel, out_shape=jax.ShapeDtypeStruct((nz, 2)...  16 us
    pallas_call x1, Pallas kernels, gather(): pl.pallas_call(functools.partial(gather_kernel, axis), out_shape=jax.Shap...  13.8 us
    unnamed x24, local copies, waits for them, and re-layouts  7.91 us

profile of v1, /device:TPU:9, one launch (start us, length us, event | category | flops | bytes accessed | tf_op | source)
XLA Modules:
  0.0 204.5 jit_solution(12962711590300432678)
XLA Ops:
  1.3 1.5 convert_reduce_fusion.1
  2.9 1.4 copy-done.2
  5.6 3.7 %dense.1 = (bf16[2048,2048]{1,0:T(8,128)(2,1)S(1)}, bf16[2048,2048]{1,0:T(8,128)(2,1)S(1)}) custom-call(s32[1,48]{1,0:T(1,128)S(1)} %copy-done.3, s32[1,48]{1,0:T(1,128)S(1)} %copy-done.4, s32[1,1]{1,0:T(1,128)S(6)} %copy.12.count_ref, bf16[48,128,128]{2,1,0:T(8,128)(2,1)S(1)} %copy-done.2), custom_call_target="tpu_custom_call" | custom-call | tf_op jit(solution)/shard_map/dense/pallas_call | solution.py:411
  9.3 3.2 %copy-done.5 = bf16[2048,2048]{1,0:T(8,128)(2,1)} copy-done((bf16[2048,2048]{1,0:T(8,128)(2,1)}, bf16[2048,2048]{1,0:T(8,128)(2,1)S(1)}, u32[]{:S(2)}) %copy-start.5) | copy-done | bytes 8388632
  13.7 3.8 %all_sum.5 = f32[24,128]{1,0:T(8,128)S(1)} custom-call(f32[24,128]{1,0:T(8,128)S(1)} %maximum_bitcast_fusion.x_ref), custom_call_target="tpu_custom_call" | custom-call | tf_op jit(solution)/shard_map/all_sum/pallas_call | solution.py:147
  17.5 1.7 fusion
  19.2 8.9 %all_sum.6 = f32[16,128]{1,0:T(8,128)S(1)} custom-call(f32[16,128]{1,0:T(8,128)S(1)} %bitcast.53), custom_call_target="tpu_custom_call" | custom-call | tf_op jit(solution)/shard_map/all_sum/pallas_call | solution.py:147
  28.1 1.7 fusion.1
  29.8 3.6 %all_sum.7 = f32[16,128]{1,0:T(8,128)S(1)} custom-call(f32[16,128]{1,0:T(8,128)S(1)} %bitcast.54), custom_call_target="tpu_custom_call" | custom-call | tf_op jit(solution)/shard_map/all_sum/pallas_call | solution.py:147
  33.5 5.2 %fusion.2 = f32[2048]{0:T(1024)S(1)} fusion(bf16[2048,2048]{1,0:T(8,128)(2,1)} %copy-done, f32[2048]{0:T(1024)S(1)} %get-tuple-element.16), kind=kLoop, calls=%fused_computation.7 | loop fusion | flops 12580864 | bytes 8404992 | tf_op jit(solution)/shard_map/reduce_sum | solution.py:429
  38.7 7.2 %all_sum.8 = f32[16,128]{1,0:T(8,128)S(1)} custom-call(f32[16,128]{1,0:T(8,128)S(1)} %bitcast.55), custom_call_target="tpu_custom_call" | custom-call | tf_op jit(solution)/shard_map/all_sum/pallas_call | solution.py:147
  46.0 1.7 fusion.3
  47.8 2.6 %fusion.5 = f32[2048,256]{1,0:T(8,128)S(1)} fusion(bf16[2048,2048]{1,0:T(8,128)(2,1)S(1)} %copy-done.1, bf16[2048,256]{1,0:T(8,128)(2,1)S(1)} %copy-done.6, f32[2048]{0:T(1024)S(1)} %divide_bitcast_fusion), kind=kOutput, calls=%fused_computation.17 | convolution fusion | flops 2149056512 | bytes 11542528 | tf_op jit(solution)/shard_map/dot_general | solution.py:469
  50.3 26.2 %scatter_sum.1 = f32[512,256]{1,0:T(8,128)S(1)} custom-call(f32[4,512,256]{2,1,0:T(8,128)S(1)} %bitcast.46), custom_call_target="tpu_custom_call" | custom-call | tf_op jit(solution)/shard_map/scatter_sum/pallas_call | solution.py:182
  76.5 3.5 %all_sum.9 = f32[16,128]{1,0:T(8,128)S(1)} custom-call(f32[16,128]{1,0:T(8,128)S(1)} %bitcast.52), custom_call_target="tpu_custom_call" | custom-call | tf_op jit(solution)/shard_map/all_sum/pallas_call | solution.py:147
  80.4 1.5 convolution_multiply_fusion.1
  82.0 20.6 %gram_sum.2 = f32[4,2,40,256]{3,2,1,0:T(8,128)S(1)} custom-call(f32[4,2,40,256]{3,2,1,0:T(8,128)S(1)} %bitcast.47), custom_call_target="tpu_custom_call" | custom-call | tf_op jit(solution)/shard_map/gram_sum/pallas_call | solution.py:373
  102.6 9.4 %inverse.2 = f32[256,256]{1,0:T(8,128)S(1)} custom-call(f32[256,256]{1,0:T(8,128)S(1)} %slice.18.gram_ref), custom_call_target="tpu_custom_call" | custom-call | tf_op jit(solution)/shard_map/inverse/pallas_call | solution.py:83
  113.0 13.8 %gather.1 = bf16[4,512,256]{2,1,0:T(8,128)(2,1)S(1)} custom-call(bf16[512,256]{1,0:T(8,128)(2,1)S(1)} %convolution_convert_fusion.x_ref), custom_call_target="tpu_custom_call" | custom-call | tf_op jit(solution)/shard_map/gather/pallas_call | solution.py:215
  127.1 2.5 %fusion.26.x_ref = f32[4,2,256,256]{3,2,1,0:T(8,128)S(1)} fusion(bf16[4,2,256,2048]{3,2,1,0:T(8,128)(2,1)S(1)} %bitcast.59, bf16[2048,256,1,1]{1,0,3,2:T(8,128)(2,1)S(1)} %bitcast.60), kind=kOutput, calls=%fused_computation.50 | convolution fusion | flops 2147483648 | bytes 11534336 | tf_op jit(solution)/shard_map/dot_general | solution.py:487
  129.6 28.4 %scatter_term.1 = f32[256,256]{1,0:T(8,128)S(1)} custom-call(f32[4,2,256,256]{3,2,1,0:T(8,128)S(1)} %fusion.26.x_ref), custom_call_target="tpu_custom_call" | custom-call | tf_op jit(solution)/shard_map/scatter_term/pallas_call | solution.py:319
  158.9 17.8 %gram_sum.3 = f32[4,2,32,256]{3,2,1,0:T(8,128)S(1)} custom-call(f32[4,2,32,256]{3,2,1,0:T(8,128)S(1)} %bitcast.51), custom_call_target="tpu_custom_call" | custom-call | tf_op jit(solution)/shard_map/gram_sum/pallas_call | solution.py:373
  176.7 9.4 %inverse.3 = f32[256,256]{1,0:T(8,128)S(1)} custom-call(f32[256,256]{1,0:T(8,128)S(1)} %bitcast.50), custom_call_target="tpu_custom_call" | custom-call | tf_op jit(solution)/shard_map/inverse/pallas_call | solution.py:83
  186.6 16.0 %gather_term.1 = bf16[4,2,256,256]{3,2,1,0:T(8,128)(2,1)S(1)} custom-call(bf16[256,256]{1,0:T(8,128)(2,1)S(1)} %convolution_convert_fusion.1.x_ref), custom_call_target="tpu_custom_call" | custom-call | tf_op jit(solution)/shard_map/gather_term/pallas_call | solution.py:337
  (45 shorter events, 7.7 us)
Async XLA Ops:
  2.9 1.4 copy-start.2
  4.3 0.7 copy-start.3
  4.9 0.7 copy-start.4
  9.3 3.2 %copy-start.5 = (bf16[2048,2048]{1,0:T(8,128)(2,1)}, bf16[2048,2048]{1,0:T(8,128)(2,1)S(1)}, u32[]{:S(2)}) copy-start(bf16[2048,2048]{1,0:T(8,128)(2,1)S(1)} %get-tuple-element.7) | copy-start | bytes 25165828
  12.5 15.6 %copy-start = (bf16[2048,2048]{1,0:T(8,128)(2,1)}, bf16[2048,2048]{1,0:T(8,128)(2,1)S(1)}, u32[]{:S(2)}) copy-start(bf16[2048,2048]{1,0:T(8,128)(2,1)S(1)} %get-tuple-element.6) | copy-start | bytes 25165828
  33.5 46.6 %copy-start.7 = (f32[2048]{0:T(1024)}, f32[2048]{0:T(1024)S(1)}, u32[]{:S(2)}) copy-start(f32[2048]{0:T(1024)S(1)} %get-tuple-element.16) | copy-start | bytes 24580
  33.5 12.5 %copy-start.1 = (bf16[2048,2048]{1,0:T(8,128)(2,1)S(1)}, bf16[2048,2048]{1,0:T(8,128)(2,1)}, u32[]{:S(2)}) copy-start(bf16[2048,2048]{1,0:T(8,128)(2,1)} %copy-done) | copy-start | bytes 25165828
  33.5 14.2 %copy-start.6 = (bf16[2048,256]{1,0:T(8,128)(2,1)S(1)}, bf16[2048,256]{1,0:T(8,128)(2,1)}, u32[]{:S(2)}) copy-start(bf16[2048,256]{1,0:T(8,128)(2,1)} %param.9) | copy-start | bytes 3145732
  45.9 4.4 %copy-start.8 = (f32[2048]{0:T(1024)}, f32[2048]{0:T(1024)S(1)}, u32[]{:S(2)}) copy-start(f32[2048]{0:T(1024)S(1)} %divide_bitcast_fusion) | copy-start | bytes 24580
  46.0 81.1 %slice-start = ((s8[8388608]{0:T(1024)(128)(4,1)}), s8[4194304]{0:T(1024)(128)(4,1)S(1)}, s32[]{:S(2)}) async-start(s8[8388608]{0:T(1024)(128)(4,1)} %bitcast.57), calls=%async_computation | async-start | bytes 8388608
  47.8 79.3 %slice-start.1 = ((s8[8388608]{0:T(1024)(128)(4,1)}), s8[4194304]{0:T(1024)(128)(4,1)S(1)}, s32[]{:S(2)}) async-start(s8[8388608]{0:T(1024)(128)(4,1)} %bitcast.57), calls=%async_computation.1 | async-start | bytes 8388608
